TPU v7x, 32 devices: a whole 2x2x4 slice. The times are simulated.
32 devices in a mesh: rel: 4 (over y, x), node: 4 (over z), feat: 2 (over core).
Axes of the slice: x: 2, y: 2, z: 4, core: 2. Of those that a mesh axis runs over, the one named last changes fastest.
Arguments:
- features: float32 [3072, 768], P('node', 'feat'), may hold values from -6 to 6
- tile_values: float32 [4, 12, 12, 256, 256], P('rel', 'node'), may hold values from -0.4375 to 0.4375
- tile_cols: int32 [4, 12, 12], P('rel', 'node'), may hold values from 0 to 11, as said below
- tile_count: int32 [4, 12], P('rel', 'node'), may hold values from 1 to 12, as said below
- degree: int32 [4, 3072], P('rel', 'node'), may hold values from 1 to 16
- proj_weight: float32 [4, 768, 512], P('rel', 'feat'), may hold values from -0.21875 to 0.21875
- proj_bias: float32 [4, 512], P('rel', 'feat'), may hold values from -3 to 3
Outputs:
- metapath_out: float32 [4, 3072, 512], P(None, ('node', 'rel'), 'feat')
Inputs may be any that keep to these rules, and one draw needn't show every extreme that they name: `tile_cols`: within one row of tiles the 12 column tiles are distinct; slots at or past the count hold valid tile numbers that are not used. `tile_count`: in every relation some row of tiles has exactly 12 live slots.
All inputs are finite; a program needn't handle non-finite values.
Results may differ from a plain program's by a relative error of at most 0.0001.
Values sent between devices are 32-bit elements; how exact they have to be, the bound alone decides.
A program may use at most 128 MiB of HBM per device.

v0:
```python
import jax
import jax.numpy as jnp
from jax import lax
from jax.sharding import PartitionSpec as P


def spread(gathered, masked, col_tiles):
    columns = gathered.shape[1]
    tile_rows = gathered.reshape(-1, masked.shape[2], columns)
    sources = jnp.take(tile_rows, col_tiles, axis=0)
    summed = jnp.einsum(
        "tkab,tkbw->taw",
        masked,
        sources,
        precision=lax.Precision.HIGH,
        preferred_element_type=jnp.float32,
    )
    return summed.reshape(-1, columns)


def on_device(features, tile_values, tile_cols, tile_count, degree, proj_weight, proj_bias):
    row_scale = lax.rsqrt(degree[0].astype(jnp.float32))[:, None]
    counts = tile_count[0]
    live_mask = (jnp.arange(tile_values.shape[2])[None, :] < counts[:, None]).astype(jnp.float32)
    masked = tile_values[0] * live_mask[:, :, None, None]
    col_tiles = tile_cols[0]
    partial_sum = jnp.dot(
        features, proj_weight[0], precision=lax.Precision.HIGH, preferred_element_type=jnp.float32
    )
    current = lax.psum_scatter(partial_sum, "feat", scatter_dimension=1, tiled=True)
    for hop_index in range(2):
        gathered = lax.all_gather(row_scale * current, "node", axis=0, tiled=True)
        current = row_scale * spread(gathered, masked, col_tiles)
    result = current + proj_bias[0][None, :]
    return lax.all_to_all(result[None], "rel", split_axis=1, concat_axis=0, tiled=True)


def solution(mesh):
    return jax.shard_map(
        on_device,
        mesh=mesh,
        in_specs=(
            P("node", "feat"),
            P("rel", "node", None, None, None),
            P("rel", "node", None),
            P("rel", "node"),
            P("rel", "node"),
            P("rel", "feat", None),
            P("rel", "feat"),
        ),
        out_specs=P(None, ("node", "rel"), "feat"),
        check_vma=False,
    )
```

profile of v0, /device:TPU:0, one launch (start us, length us, event | category | flops | bytes accessed | tf_op | source)
XLA Modules:
  0.0 216.2 jit_solution(5188851948771330307)
XLA Ops:
  6.5 1.3 copy-done
  7.8 3.7 %fusion.11 = f32[768,512]{1,0:T(8,128)} fusion(f32[768,384]{1,0:T(8,128)S(1)} %copy-done, f32[1,384,512]{2,1,0:T(8,128)} %param.14), kind=kOutput, calls=%fused_computation.15 | convolution fusion | flops 905969664 | bytes 3538944 | tf_op jit(solution)/shard_map/dot_general | solution.py:27
  11.5 0.0 reduce-scatter.2.cloned.1.call-update
  11.5 0.0 all-gather.3.cloned.1.call-start
  11.6 0.7 rsqrt_reduce_fusion
  12.3 11.1 %reduce-scatter.2.cloned.1.call-done = f32[768,256]{1,0:T(8,128)} async-done(((f32[768,512]{1,0:T(8,128)}), f32[768,256]{1,0:T(8,128)}) %reduce-scatter.2.cloned.1.call-update) | async-done | bytes 786448 | tf_op jit(solution)/shard_map/reduce_scatter | solution.py:30
  23.4 2.2 %broadcast_multiply_fusion = f32[768,256]{1,0:T(8,128)} fusion(f32[768,256]{1,0:T(8,128)} %reduce-scatter.2.cloned.1.call-done, f32[768]{0:T(1024)S(1)} %rsqrt_reduce_fusion), kind=kLoop, calls=%fused_computation.18 | loop fusion | flops 196608 | bytes 1575936 | tf_op jit(solution)/shard_map/mul | solution.py:32
  25.6 0.0 all-gather.3.cloned.1.call-update
  25.6 0.0 all-gather.5.cloned.1.call-start
  25.7 0.7 compare_select_fusion
  26.4 0.1 reshape.133
  26.5 0.8 fusion.13
  27.2 63.3 %all-gather.3.cloned.1.call-done = f32[3072,256]{1,0:T(8,128)} async-done(((f32[768,256]{1,0:T(8,128)}), f32[3072,256]{1,0:T(8,128)}) %all-gather.3.cloned.1.call-update) | async-done | bytes 3145744 | tf_op jit(solution)/shard_map/all_gather | solution.py:32
  90.5 8.6 %gather_fusion = f32[36,256,256]{2,1,0:T(8,128)} fusion(f32[12,256,256]{2,1,0:T(8,128)} %bitcast.32, s32[1024]{0:T(1024)S(1)} %pad_clamp_fusion), kind=kCustom, calls=%fused_computation.clone | custom fusion | bytes 18874512 | tf_op jit(solution)/shard_map/jit(_take)/gather | solution.py:10
  99.1 11.0 %fusion.2 = f32[3,256,256,1]{2,1,3,0:T(8,128)S(1)} fusion(f32[3,12,256,256]{3,2,1,0:T(8,128)} %bitcast.31, f32[1,3,12,256,256]{4,3,2,1,0:T(8,128)} %param.10, f32[3,12]{1,0:T(4,128)S(1)} %get-tuple-element.6, pred[3,12]{1,0:T(4,128)(4,1)S(1)} %get-tuple-element.7), kind=kOutput, calls=%fused_computation.5 | convolution fusion | flops 3628597248 | bytes 19660980 | tf_op jit(solution)/shard_map/tkab,tkbw->taw/dot_general | solution.py:11
  110.1 1.1 fusion.10
  111.1 0.0 all-gather.5.cloned.1.call-update
  111.1 62.3 %all-gather.5.cloned.1.call-done = f32[3072,256]{1,0:T(8,128)} async-done(((f32[768,256]{1,0:T(8,128)}), f32[3072,256]{1,0:T(8,128)}) %all-gather.5.cloned.1.call-update) | async-done | bytes 3145744 | tf_op jit(solution)/shard_map/all_gather | solution.py:32
  173.5 8.6 %gather_fusion.1 = f32[36,256,256]{2,1,0:T(8,128)} fusion(f32[12,256,256]{2,1,0:T(8,128)} %bitcast.33, s32[1024]{0:T(1024)S(1)} %pad_clamp_fusion), kind=kCustom, calls=%fused_computation.1.clone | custom fusion | bytes 18874512 | tf_op jit(solution)/shard_map/jit(_take)/gather | solution.py:10
  182.0 11.0 %fusion = f32[3,256,256,1]{2,1,3,0:T(8,128)S(1)} fusion(f32[3,12,256,256]{3,2,1,0:T(8,128)} %bitcast.30, f32[1,3,12,256,256]{4,3,2,1,0:T(8,128)} %param.10, f32[3,12]{1,0:T(4,128)S(1)} %get-tuple-element.6, pred[3,12]{1,0:T(4,128)(4,1)S(1)} %get-tuple-element.7), kind=kOutput, calls=%fused_computation.3 | convolution fusion | flops 3628597248 | bytes 19660980 | tf_op jit(solution)/shard_map/tkab,tkbw->taw/dot_general | solution.py:11
  193.0 0.2 multiply_add_fusion
  193.2 0.8 copy.9
  194.0 14.7 %all_to_all.12 = f32[1,768,256]{2,0,1:T(1,128)S(1)} all-to-all(f32[1,768,256]{2,0,1:T(1,128)S(1)} %copy.9), channel_id=1, replica_groups=mesh['rel'=4,'node'=4,'feat'=2] {'rel'}, dimensions={1} | all-to-all | bytes 1572864 | tf_op jit(solution)/shard_map/all_to_all | solution.py:35
  208.8 0.9 copy.13
  (5 shorter events, 0.0 us)
Async XLA Ops:
  6.5 1.3 copy-start
  6.5 16.9 %reduce-scatter.2.cloned.1.call-start = ((), (), s32[]{:S(2)}) async-start(), calls=%async_computation.2 | async-start | bytes 2359296 | tf_op jit(solution)/shard_map/reduce_scatter | solution.py:30
  11.5 79.0 %all-gather.3.cloned.1.call-start = ((), (), s32[]{:S(2)}) async-start(), calls=%async_computation.3 | async-start | bytes 3932160 | tf_op jit(solution)/shard_map/all_gather | solution.py:32
  25.6 147.8 %all-gather.5.cloned.1.call-start = ((), (), s32[]{:S(2)}) async-start(), calls=%async_computation.4 | async-start | bytes 3932160 | tf_op jit(solution)/shard_map/all_gather | solution.py:32
  182.0 11.0 %copy-start.1 = (f32[1,256]{1,0:T(1,128)S(1)}, f32[1,256]{1,0:T(1,128)}, u32[]{:S(2)}) copy-start(f32[1,256]{1,0:T(1,128)} %param.15) | copy-start | bytes 3076
Sparse Core Ops, SparseCore 0:
  11.6 11.7 reduce-scatter.1
  25.8 64.7 all-gather.2
  111.3 62.1 all-gather.4
where the time goes:
time: 217 us; the launch traced here: 216 us
  waiting for transfers between devices  137 us (63%)
  matrix products  25.6 us (12%)
  local copies, waits for them, and re-layouts  20.3 us (9%)
  blocking collectives  14.7 us (7%)
  between operations  13.2 us (6%)
  other arithmetic  5.56 us (3%)
    all_gather x2, waiting for transfers between devices, on_device(): gathered = lax.all_gather(row_scale * current, 'node', axis=0, tiled=True)  126 us
    dot_general x2, matrix products, spread(): jnp.einsum('tkab,tkbw->taw', masked, sources, precision=lax.Precision.HIG...  21.9 us
    gather x2, local copies, waits for them, and re-layouts, spread(): sources = jnp.take(tile_rows, col_tiles, axis=0)  17.2 us
    all_to_all x1, blocking collectives, on_device(): lax.all_to_all(result[None], 'rel', split_axis=1, concat_axis=0, tiled=True)  14.7 us
    reduce_scatter x1, waiting for transfers between devices, on_device(): lax.psum_scatter(partial_sum, 'feat', scatter_dimension=1, tiled=True)  11.1 us
  transfers between devices with their start and end apart: 3, of which 3 were waited for; matrix products, arithmetic and copies ran while one was open for 1% of the time, Pallas kernels for 0%

commit v1 on v0

--- a/solution.py
+++ b/solution.py
@@ -29,7 +29,26 @@
     )
     current = lax.psum_scatter(partial_sum, "feat", scatter_dimension=1, tiled=True)
     for hop_index in range(2):
-        gathered = lax.all_gather(row_scale * current, "node", axis=0, tiled=True)
+        shard = row_scale * current
+        ways, here, step = (lax.axis_size("node"), lax.axis_index("node"), shard.shape[0])
+        lengths = [n * ways if d == 0 else n for d, n in enumerate(shard.shape)]
+        full = lax.dynamic_update_slice_in_dim(
+            jnp.zeros(lengths, shard.dtype), shard, here * step, axis=0
+        )
+        going_up = going_down = shard
+        for far in range(1, ways // 2 + 1):
+            going_up = lax.ppermute(going_up, "node", [(d, (d + 1) % ways) for d in range(ways)])
+            full = lax.dynamic_update_slice_in_dim(
+                full, going_up, (here - far) % ways * step, axis=0
+            )
+            if 2 * far < ways:
+                going_down = lax.ppermute(
+                    going_down, "node", [(d, (d - 1) % ways) for d in range(ways)]
+                )
+                full = lax.dynamic_update_slice_in_dim(
+                    full, going_down, (here + far) % ways * step, axis=0
+                )
+        gathered = full
         current = row_scale * spread(gathered, masked, col_tiles)
     result = current + proj_bias[0][None, :]
     return lax.all_to_all(result[None], "rel", split_axis=1, concat_axis=0, tiled=True)

time: 217 us -> 203 us (0.935)
  waiting for transfers between devices: 137 us -> 110 us
  local copies, waits for them, and re-layouts: 20.3 us -> 29.6 us
  starting transfers between devices: 0.09 us -> 7.66 us
  other arithmetic: 5.56 us -> 3.34 us
    all_gather x2 -> x0, waiting for transfers between devices: 126 us -> none  [on_device(): gathered = lax.all_gather(row_scale * current, 'node', axis=0, tiled=True)]
    ppermute x0 -> x6, waiting for transfers between devices: none -> 97.8 us  [the longest x4 71.1 us: on_device(): lax.ppermute(going_up, 'node', [(d, (d + 1) % ways) for d in range(ways)])]
    ppermute x0 -> x6, starting transfers between devices: none -> 7.65 us  [the longest x2 5.85 us: on_device(): lax.ppermute(going_down, 'node', [(d, (d - 1) % ways) for d in range(ways)])]
    dynamic_update_slice x0 -> x6, local copies, waits for them, and re-layouts: none -> 5.63 us  [the longest x4 3.75 us: on_device(): lax.dynamic_update_slice_in_dim(full, going_up, (here - far) % ways * ste...]
    another operation x0 -> x2, local copies, waits for them, and re-layouts: none -> 3.71 us
    mul x2 -> x0, other arithmetic: 3.23 us -> none  [on_device(): gathered = lax.all_gather(row_scale * current, 'node', axis=0, tiled=True)]
    dynamic_update_slice x0 -> x2, other arithmetic: none -> 2.37 us  [on_device(): lax.dynamic_update_slice_in_dim(jnp.zeros(lengths, shard.dtype), shard, h...]
  transfers between devices with their start and end apart: 3 -> 7, of which waited for: 3 -> 7; matrix products, arithmetic and copies ran while one was open for 1% -> 2% of each run, Pallas kernels for 0% -> 0%
where the time goes in v1:
time: 203 us
  waiting for transfers between devices  110 us (54%)
  local copies, waits for them, and re-layouts  29.6 us (15%)
  matrix products  25.7 us (13%)
  blocking collectives  13.6 us (7%)
  between operations  13.5 us (7%)
  starting transfers between devices  7.66 us (4%)
  other arithmetic  3.34 us (2%)
    ppermute x4, waiting for transfers between devices, on_device(): lax.ppermute(going_up, 'node', [(d, (d + 1) % ways) for d in range(ways)])  71.1 us
    ppermute x2, waiting for transfers between devices, on_device(): lax.ppermute(going_down, 'node', [(d, (d - 1) % ways) for d in range(ways)])  26.8 us
    dot_general x2, matrix products, spread(): jnp.einsum('tkab,tkbw->taw', masked, sources, precision=lax.Precision.HIG...  22 us
    gather x2, local copies, waits for them, and re-layouts, spread(): sources = jnp.take(tile_rows, col_tiles, axis=0)  17.2 us
    all_to_all x1, blocking collectives, on_device(): lax.all_to_all(result[None], 'rel', split_axis=1, concat_axis=0, tiled=True)  13.6 us
    reduce_scatter x1, waiting for transfers between devices, on_device(): lax.psum_scatter(partial_sum, 'feat', scatter_dimension=1, tiled=True)  11.9 us
    ppermute x2, starting transfers between devices, on_device(): lax.ppermute(going_down, 'node', [(d, (d - 1) % ways) for d in range(ways)])  5.85 us
  transfers between devices with their start and end apart: 7, of which 7 were waited for; matrix products, arithmetic and copies ran while one was open for 2% of the time, Pallas kernels for 0%

profile of v1, /device:TPU:0, one launch (start us, length us, event | category | flops | bytes accessed | tf_op | source)
XLA Modules:
  0.0 203.1 jit_solution(15691735141819345578)
XLA Ops:
  6.5 1.3 copy-done
  7.8 3.7 %fusion.11 = f32[768,512]{1,0:T(8,128)} fusion(f32[768,384]{1,0:T(8,128)S(1)} %copy-done, f32[1,384,512]{2,1,0:T(8,128)} %param.14), kind=kOutput, calls=%fused_computation.15 | convolution fusion | flops 905969664 | bytes 3538944 | tf_op jit(solution)/shard_map/dot_general | solution.py:27
  11.6 11.9 %reduce-scatter.2.cloned.1.call-done = f32[768,256]{1,0:T(8,128)} async-done(((f32[768,512]{1,0:T(8,128)}), f32[768,256]{1,0:T(8,128)}) %reduce-scatter.2.cloned.1.call-update) | async-done | bytes 786448 | tf_op jit(solution)/shard_map/reduce_scatter | solution.py:30
  23.4 1.9 broadcast.56.clone
  25.3 1.3 constant_dynamic-update-slice_fusion.7
  26.6 1.8 collective-permute-start
  28.4 2.0 collective-permute-start.1
  30.4 18.6 %collective-permute-done = f32[768,256]{1,0:T(8,128)S(1)} collective-permute-done((f32[768,256]{1,0:T(8,128)}, f32[768,256]{1,0:T(8,128)S(1)}, u32[]{:S(2)}, u32[]{:S(2)}) %collective-permute-start) | collective-permute-done | bytes 786464 | tf_op jit(solution)/shard_map/ppermute | solution.py:40
  49.9 1.0 constant_dynamic-update-slice_fusion.6
  50.8 14.1 %collective-permute-done.1 = f32[768,256]{1,0:T(8,128)S(1)} collective-permute-done((f32[768,256]{1,0:T(8,128)}, f32[768,256]{1,0:T(8,128)S(1)}, u32[]{:S(2)}, u32[]{:S(2)}) %collective-permute-start.1) | collective-permute-done | bytes 786464 | tf_op jit(solution)/shard_map/ppermute | solution.py:45
  65.0 0.9 constant_dynamic-update-slice_fusion.5
  65.9 16.3 %collective-permute-done.2 = f32[768,256]{1,0:T(8,128)S(1)} collective-permute-done((f32[768,256]{1,0:T(8,128)S(1)}, f32[768,256]{1,0:T(8,128)S(1)}, u32[]{:S(2)}, u32[]{:S(2)}) %collective-permute-start.2) | collective-permute-done | bytes 786464 | tf_op jit(solution)/shard_map/ppermute | solution.py:40
  83.1 8.6 %gather_fusion = f32[36,256,256]{2,1,0:T(8,128)} fusion(f32[12,256,256]{2,1,0:T(8,128)} %bitcast.3, s32[1024]{0:T(1024)S(1)} %pad_clamp_fusion), kind=kCustom, calls=%fused_computation.clone | custom fusion | bytes 18874512 | tf_op jit(solution)/shard_map/jit(_take)/gather | solution.py:10
  91.7 11.0 %fusion.2 = f32[3,256,256,1]{2,1,3,0:T(8,128)S(1)} fusion(f32[3,12,256,256]{3,2,1,0:T(8,128)} %bitcast.31, f32[1,3,12,256,256]{4,3,2,1,0:T(8,128)} %param.10, f32[3,12]{1,0:T(4,128)S(1)} %get-tuple-element.10, pred[3,12]{1,0:T(4,128)(4,1)S(1)} %get-tuple-element.11), kind=kOutput, calls=%fused_computation.5 | convolution fusion | flops 3628597248 | bytes 19660980 | tf_op jit(solution)/shard_map/tkab,tkbw->taw/dot_general | solution.py:11
  102.7 1.9 broadcast.56
  104.5 1.1 constant_dynamic-update-slice_fusion.3
  105.6 3.8 %collective-permute-start.4 = (f32[768,256]{1,0:T(8,128)S(1)}, f32[768,256]{1,0:T(8,128)S(1)}, u32[]{:S(2)}, u32[]{:S(2)}) collective-permute-start(f32[768,256]{1,0:T(8,128)S(1)} %get-tuple-element.9), channel_id=1, source_target_pairs={{0,6},{2,0},{4,2},{6,4},{1,7},{3,1},{5,3},{7,5},{8,14},{10,8},{12,... | collective-permute-start | bytes 2359304 | tf_op jit(solution)/shard_map/ppermute | solution.py:45
  109.4 18.4 %collective-permute-done.3 = f32[768,256]{1,0:T(8,128)S(1)} collective-permute-done((f32[768,256]{1,0:T(8,128)S(1)}, f32[768,256]{1,0:T(8,128)S(1)}, u32[]{:S(2)}, u32[]{:S(2)}) %collective-permute-start.3) | collective-permute-done | bytes 786464 | tf_op jit(solution)/shard_map/ppermute | solution.py:40
  127.9 1.0 constant_dynamic-update-slice_fusion.2
  128.8 12.7 %collective-permute-done.4 = f32[768,256]{1,0:T(8,128)S(1)} collective-permute-done((f32[768,256]{1,0:T(8,128)S(1)}, f32[768,256]{1,0:T(8,128)S(1)}, u32[]{:S(2)}, u32[]{:S(2)}) %collective-permute-start.4) | collective-permute-done | bytes 786464 | tf_op jit(solution)/shard_map/ppermute | solution.py:45
  142.4 17.8 %collective-permute-done.5 = f32[768,256]{1,0:T(8,128)S(1)} collective-permute-done((f32[768,256]{1,0:T(8,128)S(1)}, f32[768,256]{1,0:T(8,128)S(1)}, u32[]{:S(2)}, u32[]{:S(2)}) %collective-permute-start.5) | collective-permute-done | bytes 786464 | tf_op jit(solution)/shard_map/ppermute | solution.py:40
  161.1 8.6 %gather_fusion.1 = f32[36,256,256]{2,1,0:T(8,128)} fusion(f32[12,256,256]{2,1,0:T(8,128)} %bitcast.8, s32[1024]{0:T(1024)S(1)} %pad_clamp_fusion), kind=kCustom, calls=%fused_computation.1.clone | custom fusion | bytes 18874512 | tf_op jit(solution)/shard_map/jit(_take)/gather | solution.py:10
  169.7 11.0 %fusion = f32[3,256,256,1]{2,1,3,0:T(8,128)S(1)} fusion(f32[3,12,256,256]{3,2,1,0:T(8,128)} %bitcast.30, f32[1,3,12,256,256]{4,3,2,1,0:T(8,128)} %param.10, f32[3,12]{1,0:T(4,128)S(1)} %get-tuple-element.10, pred[3,12]{1,0:T(4,128)(4,1)S(1)} %get-tuple-element.11), kind=kOutput, calls=%fused_computation.3 | convolution fusion | flops 3628597248 | bytes 19660980 | tf_op jit(solution)/shard_map/tkab,tkbw->taw/dot_general | solution.py:11
  181.7 13.6 %all_to_all.12 = f32[1,768,256]{2,0,1:T(1,128)S(1)} all-to-all(f32[1,768,256]{2,0,1:T(1,128)S(1)} %copy.9), channel_id=1, replica_groups=mesh['rel'=4,'node'=4,'feat'=2] {'rel'}, dimensions={1} | all-to-all | bytes 1572864 | tf_op jit(solution)/shard_map/all_to_all | solution.py:54
  (25 shorter events, 5.6 us)
Async XLA Ops:
  6.5 1.3 copy-start
  6.5 5.0 %copy-start.3 = (s32[1,768]{1,0:T(1,128)S(1)}, s32[1,768]{1,0:T(1,128)}, u32[]{:S(2)}) copy-start(s32[1,768]{1,0:T(1,128)} %param.13) | copy-start | bytes 9220
  6.5 16.9 %reduce-scatter.2.cloned.1.call-start = ((), (), s32[]{:S(2)}) async-start(), calls=%async_computation.2 | async-start | bytes 2359296 | tf_op jit(solution)/shard_map/reduce_scatter | solution.py:30
  11.5 37.5 %copy-start.2 = (s32[1,3,12]{2,0,1:T(1,128)S(1)}, s32[1,3,12]{2,0,1:T(1,128)}, u32[]{:S(2)}) copy-start(s32[1,3,12]{2,0,1:T(1,128)} %param.11) | copy-start | bytes 436
  23.4 1.9 copy-start.1
  26.6 22.4 %collective-permute-start = (f32[768,256]{1,0:T(8,128)}, f32[768,256]{1,0:T(8,128)S(1)}, u32[]{:S(2)}, u32[]{:S(2)}) collective-permute-start(f32[768,256]{1,0:T(8,128)} %get-tuple-element.7), channel_id=1, source_target_pairs={{0,2},{2,4},{4,6},{6,0},{1,3},{3,5},{5,7},{7,1},{8,10},{10,12},{12... | collective-permute-start | bytes 2359304 | tf_op jit(solution)/shard_map/ppermute | solution.py:40
  28.4 36.6 %collective-permute-start.1 = (f32[768,256]{1,0:T(8,128)}, f32[768,256]{1,0:T(8,128)S(1)}, u32[]{:S(2)}, u32[]{:S(2)}) collective-permute-start(f32[768,256]{1,0:T(8,128)} %get-tuple-element.7), channel_id=1, source_target_pairs={{0,6},{2,0},{4,2},{6,4},{1,7},{3,1},{5,3},{7,5},{8,14},{10,8},{12,... | collective-permute-start | bytes 2359304 | tf_op jit(solution)/shard_map/ppermute | solution.py:45
  49.0 33.2 %collective-permute-start.2 = (f32[768,256]{1,0:T(8,128)S(1)}, f32[768,256]{1,0:T(8,128)S(1)}, u32[]{:S(2)}, u32[]{:S(2)}) collective-permute-start(f32[768,256]{1,0:T(8,128)S(1)} %collective-permute-done), channel_id=1, source_target_pairs={{0,2},{2,4},{4,6},{6,0},{1,3},{3,5},{5,7},{7,1},{8,10},{10,12},{12... | collective-permute-start | bytes 2359304 | tf_op jit(solution)/shard_map/ppermute | solution.py:40
  105.6 22.3 %collective-permute-start.3 = (f32[768,256]{1,0:T(8,128)S(1)}, f32[768,256]{1,0:T(8,128)S(1)}, u32[]{:S(2)}, u32[]{:S(2)}) collective-permute-start(f32[768,256]{1,0:T(8,128)S(1)} %get-tuple-element.9), channel_id=1, source_target_pairs={{0,2},{2,4},{4,6},{6,0},{1,3},{3,5},{5,7},{7,1},{8,10},{10,12},{12... | collective-permute-start | bytes 2359304 | tf_op jit(solution)/shard_map/ppermute | solution.py:40
  105.6 35.9 %collective-permute-start.4 = (f32[768,256]{1,0:T(8,128)S(1)}, f32[768,256]{1,0:T(8,128)S(1)}, u32[]{:S(2)}, u32[]{:S(2)}) collective-permute-start(f32[768,256]{1,0:T(8,128)S(1)} %get-tuple-element.9), channel_id=1, source_target_pairs={{0,6},{2,0},{4,2},{6,4},{1,7},{3,1},{5,3},{7,5},{8,14},{10,8},{12,... | collective-permute-start | bytes 2359304 | tf_op jit(solution)/shard_map/ppermute | solution.py:45
  127.9 32.3 %collective-permute-start.5 = (f32[768,256]{1,0:T(8,128)S(1)}, f32[768,256]{1,0:T(8,128)S(1)}, u32[]{:S(2)}, u32[]{:S(2)}) collective-permute-start(f32[768,256]{1,0:T(8,128)S(1)} %collective-permute-done.3), channel_id=1, source_target_pairs={{0,2},{2,4},{4,6},{6,0},{1,3},{3,5},{5,7},{7,1},{8,10},{10,12},{12... | collective-permute-start | bytes 2359304 | tf_op jit(solution)/shard_map/ppermute | solution.py:40
  169.7 11.0 %copy-start.4 = (f32[1,256]{1,0:T(1,128)S(1)}, f32[1,256]{1,0:T(1,128)}, u32[]{:S(2)}) copy-start(f32[1,256]{1,0:T(1,128)} %param.15) | copy-start | bytes 3076
Sparse Core Ops, SparseCore 0:
  11.6 11.7 reduce-scatter.1
